TPU v7x, 32 devices: a whole 2x2x4 slice. The times are simulated.
32 devices in a mesh: wide: 8 (over y, x, core), narrow: 4 (over z).
Axes of the slice: x: 2, y: 2, z: 4, core: 2. Of those that a mesh axis runs over, the one named last changes fastest.
Arguments:
- pooled: bfloat16 [16384, 1024], P(('wide', 'narrow')), may hold values from -6 to 6
- cotangent: bfloat16 [16384, 512], P(('wide', 'narrow')), may hold values from -6 to 6
- w_first: bfloat16 [1024, 1024], P('narrow'), may hold values from -0.1875 to 0.1875
- b_first: float32 [1024], replicated, may hold values from -5 to 5
- w_second: bfloat16 [1024, 512], P('narrow'), may hold values from -0.1875 to 0.1875
- counts: bfloat16 [8, 64, 16384], P(None, 'narrow', 'wide'), may hold values from 0 to 3, as said below
- row_ids: int32 [8, 64], P(None, 'narrow'), may hold values from 0 to 63, as said below
- table: float32 [8, 256, 128], P(None, 'narrow'), may hold values from -6 to 6
- accum: float32 [8, 256, 128], P(None, 'narrow'), may hold values from 0.1 to 10
Outputs:
- new_table: float32 [8, 256, 128], P(None, 'narrow')
- new_accum: float32 [8, 256, 128], P(None, 'narrow')
Inputs may be any that keep to these rules, and one draw needn't show every extreme that they name: `counts`: each entry is zero where the sample does not look up the active row, else a positive lookup weight. `row_ids`: for each table, the 16 ids of one owner (slots j * 16 to (j + 1) * 16 - 1) are distinct.
All inputs are finite; a program needn't handle non-finite values.
Results may differ from a plain program's by a relative error of at most 0.0038.
Values may be sent and summed in bfloat16 or wider, within the bound.
A program may use at most 128 MiB of HBM per device.

v0:
```python
import math
import jax
import jax.numpy as jnp
from jax import lax
from jax.sharding import PartitionSpec as P

clip_factor = 0.5
learn_rate = 0.05
epsilon = 1e-08


def tower_back(inputs, cotangent, w_first, b_first, w_second):
    hidden_in = jnp.dot(inputs, w_first, preferred_element_type=jnp.float32) + b_first
    back_hidden = lax.dot_general(
        cotangent, w_second, (((1,), (1,)), ((), ())), preferred_element_type=jnp.float32
    )
    sigmoid_val = jax.nn.sigmoid(hidden_in)
    slopes = sigmoid_val * (1.0 + hidden_in * (1.0 - sigmoid_val))
    deltas = (back_hidden * slopes).astype(jnp.bfloat16)
    return lax.dot_general(
        deltas, w_first, (((1,), (1,)), ((), ())), preferred_element_type=jnp.float32
    ).astype(jnp.bfloat16)


def clip_rows(grads, limit):
    norms = jnp.sqrt(jnp.sum(grads * grads, axis=-1, keepdims=True))
    return grads * (limit / jnp.maximum(norms, limit))


def adagrad_rows(current, old_acc, summed):
    new_acc = old_acc + summed * summed
    return (current - learn_rate * summed / (jnp.sqrt(new_acc) + epsilon), new_acc)


def shards(pooled, cotangent, w_first, b_first, w_second, counts, row_ids, table, accum):
    full_first, full_second = (
        lax.all_gather(w_first, "narrow", axis=0, tiled=True),
        lax.all_gather(w_second, "narrow", axis=0, tiled=True),
    )
    grad_in = tower_back(pooled, cotangent, full_first, b_first, full_second)
    tables = counts.shape[0]
    slots = counts.shape[1]
    bags = counts.shape[2]
    emb = table.shape[2]
    samples = pooled.shape[0]
    scale = 1.0 / math.sqrt(bags)
    limit = clip_factor * math.sqrt(emb)
    regrouped = lax.all_to_all(counts, "narrow", split_axis=2, concat_axis=1, tiled=True)
    local_grad = grad_in.reshape(samples, tables, emb)
    grads = lax.psum_scatter(
        jnp.einsum(
            "tab,btd->atd", regrouped, local_grad, preferred_element_type=jnp.float32
        ).reshape(slots * lax.axis_size("narrow"), tables * emb),
        "narrow",
        scatter_dimension=0,
        tiled=True,
    ).reshape(slots, tables, emb)
    clipped = clip_rows(grads * scale, limit)
    table_index = jnp.arange(tables, dtype=jnp.int32)[:, None]
    current = jnp.transpose(table[table_index, row_ids], (1, 0, 2))
    old_acc = jnp.transpose(accum[table_index, row_ids], (1, 0, 2))
    summed = lax.psum(clipped, "wide")
    new_rows, new_acc = adagrad_rows(current, old_acc, summed)
    new_table = table.at[table_index, row_ids].set(jnp.transpose(new_rows, (1, 0, 2)))
    new_accum = accum.at[table_index, row_ids].set(jnp.transpose(new_acc, (1, 0, 2)))
    return (new_table, new_accum)


def solution(mesh):
    in_specs = (
        P(("wide", "narrow"), None),
        P(("wide", "narrow"), None),
        P("narrow", None),
        P(),
        P("narrow", None),
        P(None, "narrow", "wide"),
        P(None, "narrow"),
        P(None, "narrow", None),
        P(None, "narrow", None),
    )
    out_specs = (P(None, "narrow", None), P(None, "narrow", None))
    return jax.shard_map(shards, mesh=mesh, in_specs=in_specs, out_specs=out_specs, check_vma=False)
```

profile of v0, /device:TPU:0, one launch (start us, length us, event | category | flops | bytes accessed | tf_op | source)
XLA Modules:
  0.0 199.6 jit_solution(9209073839710677612)
XLA Ops:
  7.2 0.0 copy-start
  7.2 0.0 copy-start.3
  7.2 0.0 all-gather.5.cloned.1.call-start
  7.2 1.1 copy.53
  8.3 0.9 copy.54
  9.3 0.0 all-gather.5.cloned.1.call-update
  9.3 0.0 all-gather.3.cloned.1.call-start
  9.3 0.7 all-gather.3.cloned.1.call-update
  10.0 0.0 reduce-scatter.2.cloned.1.call-start
  10.1 0.0 copy-done.3
  10.1 4.2 %copy.26 = bf16[8,16,2048]{1,0,2:T(8,128)(2,1)} copy(bf16[8,16,2048]{2,1,0:T(8,128)(2,1)S(1)} %copy-done.3) | data formatting | bytes 1048576 | tf_op args[5]
  14.3 5.8 %reshape.51 = bf16[4,2,32768]{2,1,0:T(2,128)(2,1)S(1)} reshape(bf16[2048,8,16]{2,1,0:T(8,128)(2,1)} %bitcast.58) | data formatting | bytes 1048576
  20.1 35.4 %all_to_all.18 = bf16[4,2,32768]{2,1,0:T(2,128)(2,1)S(1)} all-to-all(bf16[4,2,32768]{2,1,0:T(2,128)(2,1)S(1)} %reshape.51), channel_id=1, replica_groups=mesh['wide'=8,'narrow'=4] {'narrow'}, dimensions={0} | all-to-all | bytes 1048576 | tf_op jit(solution)/shard_map/all_to_all | solution.py:48
  55.5 4.1 %reshape.52 = bf16[2048,8,16]{2,1,0:T(8,128)(2,1)} reshape(bf16[4,2,32768]{2,1,0:T(2,128)(2,1)S(1)} %all_to_all.18) | data formatting | bytes 1048576
  59.7 4.4 %copy.27 = bf16[8,16,4,512]{3,1,2,0:T(8,128)(2,1)S(1)} copy(bf16[8,16,4,512]{1,0,3,2:T(8,128)(2,1)} %bitcast.57) | data formatting | bytes 1048576 | tf_op jit(solution)/shard_map/all_to_all | solution.py:48
  64.1 0.0 copy-start.5
  64.1 5.2 %all-gather.5.cloned.1.call-done = bf16[1024,1024]{1,0:T(8,128)(2,1)} async-done(((bf16[256,1024]{1,0:T(8,128)(2,1)}), bf16[1024,1024]{1,0:T(8,128)(2,1)}) %all-gather.5.cloned.1.call-update) | async-done | bytes 2097168 | tf_op jit(solution)/shard_map/all_gather | solution.py:37
  69.2 0.0 copy-done
  69.2 4.2 %fusion.13 = f32[512,1024]{1,0:T(8,128)} fusion(bf16[512,1024]{1,0:T(8,128)(2,1)S(1)} %copy-done, bf16[1024,1024]{1,0:T(8,128)(2,1)} %all-gather.5.cloned.1.call-done), kind=kOutput, calls=%fused_computation.32 | convolution fusion | flops 1073741824 | bytes 5242880 | tf_op jit(solution)/shard_map/dot_general | solution.py:13
  73.4 24.1 %all-gather.3.cloned.1.call-done = bf16[1024,512]{1,0:T(8,128)(2,1)} async-done(((bf16[256,512]{1,0:T(8,128)(2,1)}), bf16[1024,512]{1,0:T(8,128)(2,1)}) %all-gather.3.cloned.1.call-update) | async-done | bytes 1048592 | tf_op jit(solution)/shard_map/all_gather | solution.py:38
  97.5 0.0 copy-done.5
  97.5 4.6 %fusion = bf16[64,8,8,128]{3,2,1,0:T(8,128)(2,1)S(1)} fusion(bf16[1024,1024]{1,0:T(8,128)(2,1)} %all-gather.5.cloned.1.call-done, f32[512,1024]{1,0:T(8,128)} %fusion.13, bf16[512,512]{1,0:T(8,128)(2,1)} %param.10, bf16[1024,512]{1,0:T(8,128)(2,1)} %all-gather.3.cloned.1.call-done, f32[1024]{0:T(1024)S(1)} %copy-done.5), kind=kOutput, calls=%fused_computation.6 | convolution fusion | flops 1616379904 | bytes 6819840 | tf_op jit(solution)/shard_map/dot_general | solution.py:20
  102.0 0.0 copy-start.4
  102.1 0.3 convolution_bitcast_fusion
  102.4 0.7 copy.47
  103.1 0.0 reduce-scatter.2.cloned.1.call-update
  103.1 0.0 all-reduce.2.cloned.1.call-start
  103.2 19.5 %reduce-scatter.2.cloned.1.call-done = f32[16,1024]{1,0:T(8,128)} async-done(((f32[64,1024]{1,0:T(8,128)}), f32[16,1024]{1,0:T(8,128)}) %reduce-scatter.2.cloned.1.call-update) | async-done | bytes 65552 | tf_op jit(solution)/shard_map/reduce_scatter | solution.py:50
  122.7 0.9 copy.35
  123.6 0.1 multiply_reduce_fusion
  123.7 0.7 bitcast_multiply_fusion
  124.4 0.0 all-reduce.2.cloned.1.call-update
  124.4 0.0 copy-done.4
  124.4 0.1 reshape.27
  124.5 1.2 gather_fusion
  125.7 1.2 gather_fusion.1
  127.0 0.1 reshape.39
  127.1 50.5 %all-reduce.2.cloned.1.call-done = f32[16,8,128]{2,1,0:T(8,128)} async-done(((f32[16,8,128]{2,1,0:T(8,128)}), f32[16,8,128]{2,1,0:T(8,128)}) %all-reduce.2.cloned.1.call-update) | async-done | bytes 65552 | tf_op jit(solution)/shard_map/psum | solution.py:62
  177.6 0.9 fusion.6
  178.6 6.9 %scatter_fusion.1 = f32[8,64,128]{2,1,0:T(8,128)S(1)} fusion(f32[8,64,128]{2,1,0:T(8,128)S(1)} %copy.54, s32[128]{0:T(128)S(1)} %reshape.39, f32[128,128]{1,0:T(8,128)S(1)} %bitcast.64), kind=kCustom, calls=%fused_computation.3 | custom fusion | bytes 197632 | tf_op jit(solution)/shard_map/scatter | solution.py:65
  185.5 0.0 copy-start.2
  185.5 6.9 %scatter_fusion = f32[8,64,128]{2,1,0:T(8,128)S(1)} fusion(f32[8,64,128]{2,1,0:T(8,128)S(1)} %copy.53, s32[128]{0:T(128)S(1)} %reshape.39, f32[128,128]{1,0:T(8,128)S(1)} %bitcast.63), kind=kCustom, calls=%fused_computation.2 | custom fusion | bytes 197632 | tf_op jit(solution)/shard_map/scatter | solution.py:64
  192.4 0.0 copy-done.2
  192.4 0.0 copy-start.1
  192.4 0.7 copy-done.1
  (5 shorter events, 0.1 us)
Async XLA Ops:
  7.2 62.1 %copy-start = (bf16[512,1024]{1,0:T(8,128)(2,1)S(1)}, bf16[512,1024]{1,0:T(8,128)(2,1)}, u32[]{:S(2)}) copy-start(bf16[512,1024]{1,0:T(8,128)(2,1)} %param.9) | copy-start | bytes 3145732
  7.2 2.9 %copy-start.3 = (bf16[8,16,2048]{2,1,0:T(8,128)(2,1)S(1)}, bf16[8,16,2048]{2,1,0:T(8,128)(2,1)}, u32[]{:S(2)}) copy-start(bf16[8,16,2048]{2,1,0:T(8,128)(2,1)} %param.14) | copy-start | bytes 1572868
  7.2 62.0 %all-gather.5.cloned.1.call-start = ((), (), s32[]{:S(2)}) async-start(), calls=%async_computation.3 | async-start | bytes 2621440 | tf_op jit(solution)/shard_map/all_gather | solution.py:37
  9.3 88.2 %all-gather.3.cloned.1.call-start = ((), (), s32[]{:S(2)}) async-start(), calls=%async_computation.2 | async-start | bytes 1310720 | tf_op jit(solution)/shard_map/all_gather | solution.py:38
  10.0 112.6 %reduce-scatter.2.cloned.1.call-start = ((), (), s32[]{:S(2)}) async-start(), calls=%async_computation.4 | async-start | bytes 327680 | tf_op jit(solution)/shard_map/reduce_scatter | solution.py:50
  64.1 33.4 %copy-start.5 = (f32[1024]{0:T(1024)S(1)}, f32[1024]{0:T(1024)}, u32[]{:S(2)}) copy-start(f32[1024]{0:T(1024)} %param.12) | copy-start | bytes 12292
  102.0 22.4 %copy-start.4 = (s32[8,16]{1,0:T(8,128)S(1)}, s32[8,16]{1,0:T(8,128)}, u32[]{:S(2)}) copy-start(s32[8,16]{1,0:T(8,128)} %param.15) | copy-start | bytes 1540
  103.1 74.5 %all-reduce.2.cloned.1.call-start = ((), (), s32[]{:S(2)}) async-start(), calls=%async_computation.5 | async-start | bytes 131072 | tf_op jit(solution)/shard_map/psum | solution.py:62
  185.5 6.9 %copy-start.2 = (f32[8,64,128]{2,1,0:T(8,128)}, f32[8,64,128]{2,1,0:T(8,128)S(1)}, u32[]{:S(2)}) copy-start(f32[8,64,128]{2,1,0:T(8,128)S(1)} %scatter_fusion.1) | copy-start | bytes 786436
  192.4 0.7 copy-start.1
Sparse Core Ops, SparseCore 0:
  9.6 59.6 all-gather.4
  70.8 26.6 all-gather.2
  103.3 19.3 reduce-scatter.1
  126.2 51.3 all-reduce.1
where the time goes:
time: 200 us
  waiting for transfers between devices  100 us (50%)
  local copies, waits for them, and re-layouts  39.3 us (20%)
  blocking collectives  35.4 us (18%)
  between operations  13.9 us (7%)
  matrix products  9.06 us (5%)
    psum x1, waiting for transfers between devices, shards(): summed = lax.psum(clipped, 'wide')  50.5 us
    all_to_all x1, blocking collectives, shards(): lax.all_to_all(counts, 'narrow', split_axis=2, concat_axis=1, tiled=True)  35.4 us
    all_gather x1, waiting for transfers between devices, shards(): lax.all_gather(w_second, 'narrow', axis=0, tiled=True)  24.1 us
    reduce_scatter x1, waiting for transfers between devices, shards(): lax.psum_scatter(jnp.einsum('tab,btd->atd', regrouped, local_grad, prefer...  19.5 us
    unnamed x18, local copies, waits for them, and re-layouts  17.7 us
    scatter x1, local copies, waits for them, and re-layouts, shards(): accum.at[table_index, row_ids].set(jnp.transpose(new_acc, (1, 0, 2)))  6.9 us
    scatter x1, local copies, waits for them, and re-layouts, shards(): table.at[table_index, row_ids].set(jnp.transpose(new_rows, (1, 0, 2)))  6.9 us
    all_gather x1, waiting for transfers between devices, shards(): lax.all_gather(w_first, 'narrow', axis=0, tiled=True)  5.15 us
  transfers between devices with their start and end apart: 4, of which 4 were waited for; matrix products, arithmetic and copies ran while one was open for 13% of the time, Pallas kernels for 0%

commit v1 on v0

--- a/solution.py
+++ b/solution.py
@@ -59,7 +59,7 @@
     table_index = jnp.arange(tables, dtype=jnp.int32)[:, None]
     current = jnp.transpose(table[table_index, row_ids], (1, 0, 2))
     old_acc = jnp.transpose(accum[table_index, row_ids], (1, 0, 2))
-    summed = lax.psum(clipped, "wide")
+    summed = jnp.sum(lax.all_gather(clipped, "wide"), axis=0)
     new_rows, new_acc = adagrad_rows(current, old_acc, summed)
     new_table = table.at[table_index, row_ids].set(jnp.transpose(new_rows, (1, 0, 2)))
     new_accum = accum.at[table_index, row_ids].set(jnp.transpose(new_acc, (1, 0, 2)))

time: 200 us -> 156 us (0.78)
  waiting for transfers between devices: 100 us -> 46.9 us
  blocking collectives: 35.4 us -> 45.3 us
    psum x1 -> x0, waiting for transfers between devices: 50.5 us -> none  [shards(): summed = lax.psum(clipped, 'wide')]
    all_gather x0 -> x1, blocking collectives: none -> 9.8 us  [shards(): summed = jnp.sum(lax.all_gather(clipped, 'wide'), axis=0)]
    reduce_scatter x1, waiting for transfers between devices: 19.5 us -> 16.9 us  [shards(): lax.psum_scatter(jnp.einsum('tab,btd->atd', regrouped, local_grad, prefer...]
    unnamed x18 -> x19, local copies, waits for them, and re-layouts: 17.7 us -> 17.7 us
  transfers between devices with their start and end apart: 4 -> 3, of which waited for: 4 -> 3; matrix products, arithmetic and copies ran while one was open for 13% -> 16% of each run, Pallas kernels for 0% -> 0%
where the time goes in v1:
time: 156 us
  waiting for transfers between devices  46.9 us (30%)
  blocking collectives  45.3 us (29%)
  local copies, waits for them, and re-layouts  39.3 us (25%)
  between operations  13.9 us (9%)
  matrix products  9.04 us (6%)
    all_to_all x1, blocking collectives, shards(): lax.all_to_all(counts, 'narrow', split_axis=2, concat_axis=1, tiled=True)  35.4 us
    all_gather x1, waiting for transfers between devices, shards(): lax.all_gather(w_second, 'narrow', axis=0, tiled=True)  24.1 us
    unnamed x19, local copies, waits for them, and re-layouts  17.7 us
    reduce_scatter x1, waiting for transfers between devices, shards(): lax.psum_scatter(jnp.einsum('tab,btd->atd', regrouped, local_grad, prefer...  16.9 us
    all_gather x1, blocking collectives, shards(): summed = jnp.sum(lax.all_gather(clipped, 'wide'), axis=0)  9.8 us
    scatter x1, local copies, waits for them, and re-layouts, shards(): accum.at[table_index, row_ids].set(jnp.transpose(new_acc, (1, 0, 2)))  6.9 us
    scatter x1, local copies, waits for them, and re-layouts, shards(): table.at[table_index, row_ids].set(jnp.transpose(new_rows, (1, 0, 2)))  6.9 us
    all_gather x1, waiting for transfers between devices, shards(): lax.all_gather(w_first, 'narrow', axis=0, tiled=True)  5.18 us
  transfers between devices with their start and end apart: 3, of which 3 were waited for; matrix products, arithmetic and copies ran while one was open for 16% of the time, Pallas kernels for 0%

profile of v1, /device:TPU:0, one launch (start us, length us, event | category | flops | bytes accessed | tf_op | source)
XLA Modules:
  0.0 155.6 jit_solution(11841349045288366326)
XLA Ops:
  7.2 0.0 copy-start
  7.2 0.0 copy-start.3
  7.2 0.0 all-gather.5.cloned.1.call-start
  7.2 1.1 copy.47
  8.3 0.9 copy.48
  9.3 0.0 all-gather.5.cloned.1.call-update
  9.3 0.0 all-gather.3.cloned.1.call-start
  9.3 0.7 all-gather.3.cloned.1.call-update
  10.0 0.0 reduce-scatter.2.cloned.1.call-start
  10.1 0.0 copy-done.3
  10.1 4.2 %copy.22 = bf16[8,16,2048]{1,0,2:T(8,128)(2,1)} copy(bf16[8,16,2048]{2,1,0:T(8,128)(2,1)S(1)} %copy-done.3) | data formatting | bytes 1048576 | tf_op args[5]
  14.3 5.8 %reshape.64 = bf16[4,2,32768]{2,1,0:T(2,128)(2,1)S(1)} reshape(bf16[2048,8,16]{2,1,0:T(8,128)(2,1)} %bitcast.55) | data formatting | bytes 1048576
  20.1 35.4 %all_to_all.18 = bf16[4,2,32768]{2,1,0:T(2,128)(2,1)S(1)} all-to-all(bf16[4,2,32768]{2,1,0:T(2,128)(2,1)S(1)} %reshape.64), channel_id=1, replica_groups=mesh['wide'=8,'narrow'=4] {'narrow'}, dimensions={0} | all-to-all | bytes 1048576 | tf_op jit(solution)/shard_map/all_to_all | solution.py:48
  55.5 4.1 %reshape.65 = bf16[2048,8,16]{2,1,0:T(8,128)(2,1)} reshape(bf16[4,2,32768]{2,1,0:T(2,128)(2,1)S(1)} %all_to_all.18) | data formatting | bytes 1048576
  59.6 4.4 %copy.23 = bf16[8,16,4,512]{3,1,2,0:T(8,128)(2,1)S(1)} copy(bf16[8,16,4,512]{1,0,3,2:T(8,128)(2,1)} %bitcast.54) | data formatting | bytes 1048576 | tf_op jit(solution)/shard_map/all_to_all | solution.py:48
  64.0 0.0 copy-start.5
  64.0 5.2 %all-gather.5.cloned.1.call-done = bf16[1024,1024]{1,0:T(8,128)(2,1)} async-done(((bf16[256,1024]{1,0:T(8,128)(2,1)}), bf16[1024,1024]{1,0:T(8,128)(2,1)}) %all-gather.5.cloned.1.call-update) | async-done | bytes 2097168 | tf_op jit(solution)/shard_map/all_gather | solution.py:37
  69.2 0.0 copy-done
  69.2 4.2 %fusion.12 = f32[512,1024]{1,0:T(8,128)} fusion(bf16[512,1024]{1,0:T(8,128)(2,1)S(1)} %copy-done, bf16[1024,1024]{1,0:T(8,128)(2,1)} %all-gather.5.cloned.1.call-done), kind=kOutput, calls=%fused_computation.30 | convolution fusion | flops 1073741824 | bytes 5242880 | tf_op jit(solution)/shard_map/dot_general | solution.py:13
  73.4 24.1 %all-gather.3.cloned.1.call-done = bf16[1024,512]{1,0:T(8,128)(2,1)} async-done(((bf16[256,512]{1,0:T(8,128)(2,1)}), bf16[1024,512]{1,0:T(8,128)(2,1)}) %all-gather.3.cloned.1.call-update) | async-done | bytes 1048592 | tf_op jit(solution)/shard_map/all_gather | solution.py:38
  97.5 0.0 copy-done.5
  97.5 4.6 %fusion = bf16[64,8,8,128]{3,2,1,0:T(8,128)(2,1)S(1)} fusion(bf16[1024,1024]{1,0:T(8,128)(2,1)} %all-gather.5.cloned.1.call-done, f32[512,1024]{1,0:T(8,128)} %fusion.12, bf16[512,512]{1,0:T(8,128)(2,1)} %param.10, bf16[1024,512]{1,0:T(8,128)(2,1)} %all-gather.3.cloned.1.call-done, f32[1024]{0:T(1024)S(1)} %copy-done.5), kind=kOutput, calls=%fused_computation.6 | convolution fusion | flops 1616379904 | bytes 6819840 | tf_op jit(solution)/shard_map/dot_general | solution.py:20
  102.0 0.0 copy-start.4
  102.1 0.3 convolution_bitcast_fusion
  102.4 0.7 copy.42
  103.1 0.0 reduce-scatter.2.cloned.1.call-update
  103.1 0.0 copy-done.4
  103.2 0.1 reshape.40
  103.2 1.2 gather_fusion
  104.5 1.2 gather_fusion.1
  105.7 0.1 reshape.52
  105.8 16.9 %reduce-scatter.2.cloned.1.call-done = f32[16,1024]{1,0:T(8,128)} async-done(((f32[64,1024]{1,0:T(8,128)}), f32[16,1024]{1,0:T(8,128)}) %reduce-scatter.2.cloned.1.call-update) | async-done | bytes 65552 | tf_op jit(solution)/shard_map/reduce_scatter | solution.py:50
  122.7 0.8 multiply_bitcast_fusion
  123.5 0.1 reduce_sum.18
  123.7 0.9 copy.32
  124.5 0.1 bitcast_multiply_fusion
  124.6 9.8 %all_gather.12 = f32[8,16,8,128]{3,2,1,0:T(8,128)S(1)} all-gather(f32[1,16,8,128]{3,2,1,0:T(8,128)S(1)} %bitcast_multiply_fusion), channel_id=1, replica_groups=mesh['wide'=8,'narrow'=4] {'wide'}, dimensions={0}, use_global_device_ids=true | all-gather | bytes 589824 | tf_op jit(solution)/shard_map/all_gather | solution.py:62
  134.4 0.1 fusion.5
  134.6 6.9 %scatter_fusion.1 = f32[8,64,128]{2,1,0:T(8,128)S(1)} fusion(f32[8,64,128]{2,1,0:T(8,128)S(1)} %copy.48, s32[128]{0:T(128)S(1)} %reshape.52, f32[128,128]{1,0:T(8,128)S(1)} %bitcast.61), kind=kCustom, calls=%fused_computation.3 | custom fusion | bytes 197632 | tf_op jit(solution)/shard_map/scatter | solution.py:65
  141.5 0.0 copy-start.2
  141.5 6.9 %scatter_fusion = f32[8,64,128]{2,1,0:T(8,128)S(1)} fusion(f32[8,64,128]{2,1,0:T(8,128)S(1)} %copy.47, s32[128]{0:T(128)S(1)} %reshape.52, f32[128,128]{1,0:T(8,128)S(1)} %bitcast.60), kind=kCustom, calls=%fused_computation.2 | custom fusion | bytes 197632 | tf_op jit(solution)/shard_map/scatter | solution.py:64
  148.4 0.0 copy-done.2
  148.4 0.0 copy-start.1
  148.4 0.7 copy-done.1
  (6 shorter events, 0.1 us)
Async XLA Ops:
  7.2 62.1 %copy-start = (bf16[512,1024]{1,0:T(8,128)(2,1)S(1)}, bf16[512,1024]{1,0:T(8,128)(2,1)}, u32[]{:S(2)}) copy-start(bf16[512,1024]{1,0:T(8,128)(2,1)} %param.9) | copy-start | bytes 3145732
  7.2 2.9 %copy-start.3 = (bf16[8,16,2048]{2,1,0:T(8,128)(2,1)S(1)}, bf16[8,16,2048]{2,1,0:T(8,128)(2,1)}, u32[]{:S(2)}) copy-start(bf16[8,16,2048]{2,1,0:T(8,128)(2,1)} %param.14) | copy-start | bytes 1572868
  7.2 62.0 %all-gather.5.cloned.1.call-start = ((), (), s32[]{:S(2)}) async-start(), calls=%async_computation.3 | async-start | bytes 2621440 | tf_op jit(solution)/shard_map/all_gather | solution.py:37
  9.3 88.2 %all-gather.3.cloned.1.call-start = ((), (), s32[]{:S(2)}) async-start(), calls=%async_computation.2 | async-start | bytes 1310720 | tf_op jit(solution)/shard_map/all_gather | solution.py:38
  10.0 112.6 %reduce-scatter.2.cloned.1.call-start = ((), (), s32[]{:S(2)}) async-start(), calls=%async_computation.4 | async-start | bytes 327680 | tf_op jit(solution)/shard_map/reduce_scatter | solution.py:50
  64.0 33.5 %copy-start.5 = (f32[1024]{0:T(1024)S(1)}, f32[1024]{0:T(1024)}, u32[]{:S(2)}) copy-start(f32[1024]{0:T(1024)} %param.12) | copy-start | bytes 12292
  102.0 1.1 copy-start.4
  141.5 6.9 %copy-start.2 = (f32[8,64,128]{2,1,0:T(8,128)}, f32[8,64,128]{2,1,0:T(8,128)S(1)}, u32[]{:S(2)}) copy-start(f32[8,64,128]{2,1,0:T(8,128)S(1)} %scatter_fusion.1) | copy-start | bytes 786436
  148.4 0.7 copy-start.1
Sparse Core Ops, SparseCore 0:
  9.6 59.6 all-gather.4
  70.8 26.6 all-gather.2
  103.3 19.3 reduce-scatter.1
